TPU v7x, 32 devices: a whole 2x2x4 slice. The times are simulated.
32 devices in a mesh: sp: 8 (over z, y), tp: 4 (over x, core).
Axes of the slice: x: 2, y: 2, z: 4, core: 2. Of those that a mesh axis runs over, the one named last changes fastest.
Arguments:
- patches: float32 [160, 240, 256], P('sp', None, 'tp'), may hold values from -6 to 6
- merge_gain: float32 [4, 256], P(None, 'tp'), may hold values from 0.25 to 1.75
- merge_shift: float32 [4, 256], P(None, 'tp'), may hold values from -1.75 to 1.75
- merge_weight: float32 [4, 256, 512], P(None, 'tp'), may hold values from -0.1875 to 0.1875
- first_gain: float32 [2, 512], replicated, may hold values from 0.25 to 1.75
- first_shift: float32 [2, 512], replicated, may hold values from -1.75 to 1.75
- input_weight: float32 [2, 512, 3, 512], P(None, None, None, 'tp'), may hold values from -0.375 to 0.375
- input_bias: float32 [2, 2, 512], P(None, None, 'tp'), may hold values from -1.75 to 1.75
- position_table: float32 [2, 361, 16], P(None, None, 'tp'), may hold values from -6 to 6
- output_weight: float32 [2, 512, 512], P(None, 'tp'), may hold values from -0.75 to 0.75
- output_bias: float32 [2, 512], replicated, may hold values from -1.75 to 1.75
- second_gain: float32 [2, 512], replicated, may hold values from 0.25 to 1.75
- second_shift: float32 [2, 512], replicated, may hold values from -1.75 to 1.75
- expand_weight: float32 [2, 512, 2048], P(None, None, 'tp'), may hold values from -0.25 to 0.25
- expand_bias: float32 [2, 2048], P(None, 'tp'), may hold values from -1.75 to 1.75
- shrink_weight: float32 [2, 2048, 512], P(None, 'tp'), may hold values from -0.1875 to 0.1875
- shrink_bias: float32 [2, 512], replicated, may hold values from -1.75 to 1.75
- page_map: int32 [8, 12], replicated, may hold values from 0 to 58, as said below
- valid_flags: int32 [80, 120], P('sp'), may hold values from 0 to 1, as said below
- cotangent: float32 [80, 120, 512], P('sp', None, 'tp'), may hold values from -6 to 6
Outputs:
- output: float32 [80, 120, 512], P('sp', None, 'tp')
- patches_grad: float32 [160, 240, 256], P('sp', None, 'tp')
- merge_gain_grad: float32 [4, 256], P(None, 'tp')
- merge_shift_grad: float32 [4, 256], P(None, 'tp')
- merge_weight_grad: float32 [4, 256, 512], P(None, 'tp')
- first_gain_grad: float32 [2, 512], replicated
- first_shift_grad: float32 [2, 512], replicated
- input_weight_grad: float32 [2, 512, 3, 512], P(None, None, None, 'tp')
- input_bias_grad: float32 [2, 2, 512], P(None, None, 'tp')
- position_table_grad: float32 [2, 361, 16], P(None, None, 'tp')
- output_weight_grad: float32 [2, 512, 512], P(None, 'tp')
- output_bias_grad: float32 [2, 512], replicated
- second_gain_grad: float32 [2, 512], replicated
- second_shift_grad: float32 [2, 512], replicated
- expand_weight_grad: float32 [2, 512, 2048], P(None, None, 'tp')
- expand_bias_grad: float32 [2, 2048], P(None, 'tp')
- shrink_weight_grad: float32 [2, 2048, 512], P(None, 'tp')
- shrink_bias_grad: float32 [2, 512], replicated
- rms: float32 [5], replicated
Inputs may be any that keep to these rules, and one draw needn't show every extreme that they name: `page_map`: the windows of one page form a rectangle of whole windows; pages are numbered row_page * 13 + column_page, both never falling along their axis, starting at 0 in the first window, with exactly 4 row breaks and 6 column breaks, so the last window holds the largest number. `valid_flags`: the first patch of every window is valid.
All inputs are finite; a program needn't handle non-finite values.
Results may differ from a plain program's by a relative error of at most 0.0003.
Values sent between devices are 32-bit elements; how exact they have to be, the bound alone decides.
A program may use at most 192 MiB of HBM per device.

v0:
```python
import jax
import jax.numpy as jnp
from jax import lax
from jax.sharding import PartitionSpec as P

C = 512
HD = 32
C2 = 256
WIN = 10
SHIFT = 5
highest = lax.Precision.HIGHEST
epsilon = 1e-05
masked = -1000000000.0


def passed_along(block, axis, distance):
    devices = range(lax.axis_size(axis))
    route = [((i - distance) % len(devices), i) for i in devices]
    return lax.ppermute(block, axis, route)


def layer_norm(values, gain_row, offset):
    center = values - jnp.mean(values, axis=-1, keepdims=True)
    spread = jnp.mean(center * center, axis=-1, keepdims=True)
    return center * lax.rsqrt(spread + epsilon) * gain_row + offset


def exact_gelu(values):
    return jax.nn.gelu(values, approximate=False)


def relative_index():
    positions = jnp.arange(WIN * WIN, dtype=jnp.int32)
    row_of = positions // WIN
    column_of = positions % WIN
    row_offset = row_of[:, None] - row_of[None, :] + (WIN - 1)
    column_offset = column_of[:, None] - column_of[None, :] + (WIN - 1)
    return row_offset * (2 * WIN - 1) + column_offset


def window_attention(queries, key_rows, value_rows, bias_grid, region, validity):
    scores = (
        jnp.einsum("wqhd,wkhd->whqk", queries, key_rows, precision=highest) * HD ** (-0.5)
        + bias_grid[None]
    )
    same_region = region[:, :, None] == region[:, None, :]
    diagonal = jnp.eye(WIN * WIN, dtype=bool)[None]
    allowed = same_region & (validity[:, None, :] > 0) | diagonal
    scores = jnp.where(allowed[:, None], scores, masked)
    row_max = jnp.max(scores, axis=-1, keepdims=True)
    weights = jnp.exp(scores - row_max)
    weights = weights / jnp.sum(weights, axis=-1, keepdims=True)
    return jnp.einsum("whqk,wkhd->wqhd", weights, value_rows, precision=highest)


def to_windows(values):
    row_count, column_count = (values.shape[0], values.shape[1])
    trailing = values.shape[2:]
    windowed = values.reshape((row_count // WIN, WIN, column_count // WIN, WIN) + trailing)
    windowed = jnp.moveaxis(windowed, 2, 1)
    return windowed.reshape((row_count // WIN, column_count // WIN, WIN * WIN) + trailing)


def from_windows(windowed, row_count, column_count):
    trailing = windowed.shape[3:]
    values = windowed.reshape((row_count // WIN, column_count // WIN, WIN, WIN) + trailing)
    values = jnp.moveaxis(values, 1, 2)
    return values.reshape((row_count, column_count) + trailing)


def local_attention(window_grid, key_valid, region, table_here, bias_index):
    row_count, column_count = key_valid.shape
    window_count = row_count // WIN * (column_count // WIN)
    local_heads = table_here.shape[1]
    windowed = to_windows(window_grid).reshape(window_count, WIN * WIN, 3, local_heads, HD)
    bias_grid = jnp.transpose(table_here[bias_index], (2, 0, 1))
    attended = window_attention(
        windowed[:, :, 0],
        windowed[:, :, 1],
        windowed[:, :, 2],
        bias_grid,
        to_windows(region).reshape(window_count, WIN * WIN),
        to_windows(key_valid).reshape(window_count, WIN * WIN),
    )
    attended = attended.reshape(row_count // WIN, column_count // WIN, WIN * WIN, local_heads * HD)
    return from_windows(attended, row_count, column_count)


def shifted_region(page_map, sp_index, row_count, column_count, sp_count):
    total_rows = row_count * sp_count
    local_rows = jnp.arange(row_count, dtype=jnp.int32)[:, None]
    root_row = (sp_index * row_count + local_rows + SHIFT) % total_rows
    root_column = (jnp.arange(column_count, dtype=jnp.int32)[None, :] + SHIFT) % column_count
    flat_index = root_row // WIN * page_map.shape[1] + root_column // WIN
    page = jnp.take(page_map.reshape(-1), flat_index)
    wrap_row = (root_row < SHIFT).astype(jnp.int32)
    wrap_column = (root_column < SHIFT).astype(jnp.int32)
    return page * 4 + wrap_row * 2 + wrap_column


def branch_total(partial_value):
    return lax.psum(partial_value, "tp")


def input_total(partial_value):
    return lax.psum(partial_value, "tp")


def shards(
    patches,
    merge_gain,
    merge_shift,
    merge_weight,
    first_gain,
    first_shift,
    input_weight,
    input_bias,
    position_table,
    output_weight,
    output_bias,
    second_gain,
    second_shift,
    expand_weight,
    expand_bias,
    shrink_weight,
    shrink_bias,
    page_map,
    valid_flags,
    cotangent,
):
    row_count, column_count = valid_flags.shape
    tokens = row_count * column_count
    tp_index = lax.axis_index("tp")
    sp_index = lax.axis_index("sp")
    local_width = output_weight.shape[1]
    valid_float = valid_flags.astype(jnp.float32)
    valid_column = valid_float.reshape(tokens, 1)
    bias_index = relative_index()
    region_flat = jnp.zeros((row_count, column_count), jnp.int32)
    region_moved = shifted_region(page_map, sp_index, row_count, column_count, lax.axis_size("sp"))
    full_channels = 4 * C2
    quads = (
        patches.reshape(row_count, 2, column_count, 2, -1)
        .transpose(0, 2, 3, 1, 4)
        .reshape(tokens, 4, -1)
    )
    moments = lax.psum((jnp.sum(quads, axis=(1, 2)), jnp.sum(quads * quads, axis=(1, 2))), "tp")
    center_mean = moments[0] / full_channels
    inverse = lax.rsqrt(moments[1] / full_channels - center_mean * center_mean + epsilon)
    centered = (quads - center_mean[:, None, None]) * inverse[:, None, None]
    merged = centered * merge_gain + merge_shift
    field = branch_total(jnp.einsum("tkc,kcd->td", merged, merge_weight, precision=highest))
    stored = []
    square_list = []
    for block_index in range(2):
        shifted_block = block_index == 1
        normed = layer_norm(field, first_gain[block_index], first_shift[block_index])
        projected = jnp.einsum("td,dkf->tkf", normed, input_weight[block_index], precision=highest)
        bias_rows = jnp.stack(
            [
                input_bias[block_index, 0],
                jnp.zeros_like(input_bias[block_index, 0]),
                input_bias[block_index, 1],
            ]
        )
        window_grid = (projected + bias_rows).reshape(row_count, column_count, 3 * local_width)
        if shifted_block:
            top_rows = passed_along((window_grid[:SHIFT], valid_float[:SHIFT]), "sp", -1)
            window_grid = jnp.roll(
                jnp.concatenate([window_grid[SHIFT:], top_rows[0]], 0), -SHIFT, axis=1
            )
            key_valid = jnp.roll(
                jnp.concatenate([valid_float[SHIFT:], top_rows[1]], 0), -SHIFT, axis=1
            )
            region = region_moved
        else:
            key_valid = valid_float
            region = region_flat
        attended = local_attention(
            window_grid, key_valid, region, position_table[block_index], bias_index
        )
        if shifted_block:
            turned = jnp.roll(attended, SHIFT, axis=1)
            carried = passed_along(turned[row_count - SHIFT :], "sp", 1)
            attended = jnp.concatenate([carried, turned[: row_count - SHIFT]], 0)
        attended = attended.reshape(tokens, local_width)
        mixed_out = (
            branch_total(jnp.dot(attended, output_weight[block_index], precision=highest))
            + output_bias[block_index]
        )
        middle = field + mixed_out
        normed_two = layer_norm(middle, second_gain[block_index], second_shift[block_index])
        pre_act = (
            jnp.dot(normed_two, expand_weight[block_index], precision=highest)
            + expand_bias[block_index]
        )
        hidden = exact_gelu(pre_act)
        branch = (
            branch_total(jnp.dot(hidden, shrink_weight[block_index], precision=highest))
            + shrink_bias[block_index]
        )
        stored.append(
            (
                field,
                normed,
                window_grid,
                key_valid,
                region,
                attended,
                middle,
                normed_two,
                pre_act,
                hidden,
            )
        )
        square_list.append(jnp.sum(mixed_out * mixed_out * valid_column))
        square_list.append(jnp.sum(branch * branch * valid_column))
        field = middle + branch
    square_list.append(jnp.sum(field * field * valid_column))
    square_sums = jnp.stack(square_list)
    valid_count = jnp.sum(valid_float)
    output = lax.dynamic_slice_in_dim(
        field.reshape(row_count, column_count, C), tp_index * local_width, local_width, 2
    )

    def block_backward(block_index, grad_field):
        (
            field_in,
            normed,
            window_grid,
            key_valid,
            region,
            attended,
            middle,
            normed_two,
            pre_act,
            hidden,
        ) = stored[block_index]
        shrink_bias_g = jnp.sum(grad_field, axis=0)
        shrink_weight_g = jnp.dot(hidden.T, grad_field, precision=highest)
        grad_hidden = jnp.dot(grad_field, shrink_weight[block_index].T, precision=highest)
        grad_pre = jax.vjp(exact_gelu, pre_act)[1](grad_hidden)[0]
        expand_bias_g = jnp.sum(grad_pre, axis=0)
        expand_weight_g = jnp.dot(normed_two.T, grad_pre, precision=highest)
        grad_normed_two = input_total(
            jnp.dot(grad_pre, expand_weight[block_index].T, precision=highest)
        )
        pull_second = jax.vjp(
            layer_norm, middle, second_gain[block_index], second_shift[block_index]
        )[1]
        grad_inner, second_gain_g, second_shift_g = pull_second(grad_normed_two)
        grad_middle = grad_field + grad_inner
        output_bias_g = jnp.sum(grad_middle, axis=0)
        output_weight_g = jnp.dot(attended.T, grad_middle, precision=highest)
        grad_attended = jnp.dot(
            grad_middle, output_weight[block_index].T, precision=highest
        ).reshape(row_count, column_count, local_width)
        if block_index == 1:
            upper_rows = passed_along(grad_attended[:SHIFT], "sp", -1)
            grad_attended = jnp.roll(
                jnp.concatenate([grad_attended[SHIFT:], upper_rows], 0), -SHIFT, axis=1
            )

        def attend(grid_in, table_in):
            return local_attention(grid_in, key_valid, region, table_in, bias_index)

        pull_attention = jax.vjp(attend, window_grid, position_table[block_index])[1]
        grad_grid, table_g = pull_attention(grad_attended)
        if block_index == 1:
            turned = jnp.roll(grad_grid, SHIFT, axis=1)
            lower_rows = passed_along(turned[row_count - SHIFT :], "sp", 1)
            grad_grid = jnp.concatenate([lower_rows, turned[: row_count - SHIFT]], 0)
        grad_projected = grad_grid.reshape(tokens, 3, local_width)
        input_bias_g = jnp.stack(
            [jnp.sum(grad_projected[:, 0], axis=0), jnp.sum(grad_projected[:, 2], axis=0)]
        )
        input_weight_g = jnp.einsum("td,tkf->dkf", normed, grad_projected, precision=highest)
        grad_normed = input_total(
            jnp.einsum("tkf,dkf->td", grad_projected, input_weight[block_index], precision=highest)
        )
        pull_first = jax.vjp(
            layer_norm, field_in, first_gain[block_index], first_shift[block_index]
        )[1]
        grad_outer, first_gain_g, first_shift_g = pull_first(grad_normed)
        grads_here = (
            first_gain_g,
            first_shift_g,
            input_weight_g,
            input_bias_g,
            table_g,
            output_weight_g,
            output_bias_g,
            second_gain_g,
            second_shift_g,
            expand_weight_g,
            expand_bias_g,
            shrink_weight_g,
            shrink_bias_g,
        )
        return (grad_middle + grad_outer, grads_here)

    grad_field = lax.all_gather(cotangent, "tp", axis=2, tiled=True).reshape(tokens, C)
    grad_field, late_grads = block_backward(1, grad_field)
    grad_field, early_grads = block_backward(0, grad_field)
    merge_weight_g = jnp.einsum("tkc,td->kcd", merged, grad_field, precision=highest)
    grad_merged = jnp.einsum("td,kcd->tkc", grad_field, merge_weight, precision=highest)
    merge_gain_g = jnp.sum(grad_merged * centered, axis=0)
    merge_shift_g = jnp.sum(grad_merged, axis=0)
    grad_hat = grad_merged * merge_gain
    back_moments = lax.psum(
        (jnp.sum(grad_hat, axis=(1, 2)), jnp.sum(grad_hat * centered, axis=(1, 2))), "tp"
    )
    grad_quads = inverse[:, None, None] * (
        grad_hat
        - back_moments[0][:, None, None] / full_channels
        - centered * back_moments[1][:, None, None] / full_channels
    )
    patches_grad = (
        grad_quads.reshape(row_count, column_count, 2, 2, -1)
        .transpose(0, 3, 1, 2, 4)
        .reshape(2 * row_count, 2 * column_count, -1)
    )
    whole_total = lax.psum(
        (
            early_grads[0],
            early_grads[1],
            early_grads[2],
            early_grads[3],
            early_grads[4],
            early_grads[5],
            early_grads[6],
            early_grads[7],
            early_grads[8],
            early_grads[9],
            early_grads[10],
            early_grads[11],
            early_grads[12],
            late_grads[0],
            late_grads[1],
            late_grads[2],
            late_grads[3],
            late_grads[4],
            late_grads[5],
            late_grads[6],
            late_grads[7],
            late_grads[8],
            late_grads[9],
            late_grads[10],
            late_grads[11],
            late_grads[12],
            merge_gain_g,
            merge_shift_g,
            merge_weight_g,
            square_sums,
            valid_count,
        ),
        "sp",
    )
    early_grads = whole_total[:13]
    late_grads = whole_total[13:26]
    merge_gain_g = whole_total[26]
    merge_shift_g = whole_total[27]
    merge_weight_g = whole_total[28]
    square_sums = whole_total[29]
    valid_count = whole_total[30]
    stacked = [jnp.stack([early_grads[position], late_grads[position]]) for position in range(13)]
    rms = jnp.sqrt(square_sums / (valid_count * C))
    return (
        output,
        patches_grad,
        merge_gain_g,
        merge_shift_g,
        merge_weight_g,
        stacked[0],
        stacked[1],
        stacked[2],
        stacked[3],
        stacked[4],
        stacked[5],
        stacked[6],
        stacked[7],
        stacked[8],
        stacked[9],
        stacked[10],
        stacked[11],
        stacked[12],
        rms,
    )


def solution(mesh):
    placed = (
        P("sp", None, "tp"),
        P(None, "tp"),
        P(None, "tp"),
        P(None, "tp", None),
        P(),
        P(),
        P(None, None, None, "tp"),
        P(None, None, "tp"),
        P(None, None, "tp"),
        P(None, "tp", None),
        P(),
        P(),
        P(),
        P(None, None, "tp"),
        P(None, "tp"),
        P(None, "tp", None),
        P(),
        P(),
        P("sp", None),
        P("sp", None, "tp"),
    )
    return jax.shard_map(
        shards,
        mesh=mesh,
        in_specs=placed,
        out_specs=(
            P("sp", None, "tp"),
            P("sp", None, "tp"),
            P(None, "tp"),
            P(None, "tp"),
            P(None, "tp", None),
            P(),
            P(),
            P(None, None, None, "tp"),
            P(None, None, "tp"),
            P(None, None, "tp"),
            P(None, "tp", None),
            P(),
            P(),
            P(),
            P(None, None, "tp"),
            P(None, "tp"),
            P(None, "tp", None),
            P(),
            P(),
        ),
        check_vma=False,
    )
```

profile of v0, /device:TPU:0, one launch (start us, length us, event | category | flops | bytes accessed | tf_op | source)
XLA Modules:
  0.0 1262.3 jit_solution(3288617347281952883)
XLA Ops:
  8.6 6.0 collective-permute-start.1
  16.5 6.9 fusion.220
  29.1 10.6 all-reduce.9
  47.4 7.3 gather_fusion.1
  56.2 19.6 %gather_fusion = f32[10000,4]{1,0:T(8,128)} fusion(f32[361,4]{1,0:T(8,128)S(1)} %bitcast.327, s32[10240]{0:T(1024)S(1)} %pad_clamp_fusion), kind=kCustom, calls=%fused_computation | custom fusion | bytes 360000 | tf_op jit(solution)/shard_map/gather | solution.py:76
  82.7 16.0 %all-reduce.21.cloned.1.call-done = f32[1200,512]{1,0:T(8,128)} async-done(((f32[1200,512]{1,0:T(8,128)}), f32[1200,512]{1,0:T(8,128)}) %all-reduce.21.cloned.1.call-update) | async-done | bytes 2457616 | tf_op jit(solution)/shard_map/psum | solution.py:102
  117.2 6.9 reshape_reshape.21
  124.1 7.1 fusion.234
  138.7 5.9 fusion.246
  161.8 54.7 %all-reduce.23.cloned.1.call-done = f32[1200,512]{1,0:T(8,128)} async-done(((f32[1200,512]{1,0:T(8,128)}), f32[1200,512]{1,0:T(8,128)}) %all-reduce.23.cloned.1.call-update) | async-done | bytes 2457616 | tf_op jit(solution)/shard_map/psum | solution.py:102
  220.8 9.4 fusion
  232.6 5.8 fusion.120
  239.7 56.2 %all-reduce.25.cloned.1.call-done = f32[1200,512]{1,0:T(8,128)} async-done(((f32[1200,512]{1,0:T(8,128)}), f32[1200,512]{1,0:T(8,128)}) %all-reduce.25.cloned.1.call-update) | async-done | bytes 2457616 | tf_op jit(solution)/shard_map/psum | solution.py:102
  313.9 19.6 %gather_fusion.2 = f32[10000,4]{1,0:T(8,128)} fusion(f32[361,4]{1,0:T(8,128)S(1)} %bitcast.326, s32[10240]{0:T(1024)S(1)} %pad_clamp_fusion), kind=kCustom, calls=%fused_computation.2 | custom fusion | bytes 360000 | tf_op jit(solution)/shard_map/gather | solution.py:76
  353.2 6.8 reshape_reshape.24
  360.0 6.3 fusion.233
  375.3 5.9 fusion.247
  398.7 11.3 collective-permute-done.2
  416.4 53.2 %all-reduce.27.cloned.1.call-done = f32[1200,512]{1,0:T(8,128)} async-done(((f32[1200,512]{1,0:T(8,128)}), f32[1200,512]{1,0:T(8,128)}) %all-reduce.27.cloned.1.call-update) | async-done | bytes 2457616 | tf_op jit(solution)/shard_map/psum | solution.py:102
  474.8 11.0 fusion.1
  485.9 10.1 all-gather.2.cloned.1.call-done
  496.0 9.2 fusion.248
  512.6 57.1 %all-reduce.29.cloned.1.call-done = f32[1200,512]{1,0:T(8,128)} async-done(((f32[1200,512]{1,0:T(8,128)}), f32[1200,512]{1,0:T(8,128)}) %all-reduce.29.cloned.1.call-update) | async-done | bytes 2457616 | tf_op jit(solution)/shard_map/psum | solution.py:106
  583.6 5.8 collective-permute-done.3
  601.3 6.2 convolution_bitcast_fusion.7
  623.6 7.1 copy.141
  630.6 7.3 reshape.689
  648.1 24.0 %collective-permute-done.4 = f32[5,120,384]{2,1,0:T(8,128)S(1)} collective-permute-done((f32[5,120,384]{2,1,0:T(8,128)S(1)}, f32[5,120,384]{2,1,0:T(8,128)S(1)}, u32[]{:S(2)}, u32[]{:S(2)}) %collective-permute-start.4) | collective-permute-done | bytes 921632 | tf_op jit(solution)/shard_map/ppermute | solution.py:19
  677.5 7.4 convolution_bitcast_fusion.2
  685.2 55.1 %all-reduce.31.cloned.1.call-done = f32[1200,512]{1,0:T(8,128)} async-done(((f32[1200,512]{1,0:T(8,128)}), f32[1200,512]{1,0:T(8,128)}) %all-reduce.31.cloned.1.call-update) | async-done | bytes 2457616 | tf_op jit(solution)/shard_map/psum | solution.py:106
  763.7 8.3 fusion.111
  772.0 48.1 %all-reduce.33.cloned.1.call-done = f32[1200,512]{1,0:T(8,128)} async-done(((f32[1200,512]{1,0:T(8,128)}), f32[1200,512]{1,0:T(8,128)}) %all-reduce.33.cloned.1.call-update) | async-done | bytes 2457616 | tf_op jit(solution)/shard_map/psum | solution.py:106
  844.6 6.2 convolution_bitcast_fusion.6
  866.9 7.1 copy.150
  874.0 7.3 reshape.694
  889.4 7.4 convolution_bitcast_fusion.1
  897.6 8.4 fusion.49
  906.0 7.4 convolution_bitcast_fusion.3
  915.9 6.0 fusion.56
  921.9 5.9 fusion.50
  936.1 5.8 fusion.51
  942.0 52.5 %all-reduce.37.cloned.1.call-done = (f32[1200,512]{1,0:T(8,128)}, f32[1200,512]{1,0:T(8,128)}) async-done(((f32[1200,512]{1,0:T(8,128)}, f32[1200,512]{1,0:T(8,128)}), (f32[1200,512]{1,0:T(8,128)}, f32[1200,512]{1,0:T(8,128)})) %all-reduce.37.cloned.1.call-update) | async-done | bytes 4915216 | tf_op jit(solution)/shard_map/psum | solution.py:102
  1016.9 56.0 %scatter_custom_fusion.1 = f32[361,4]{1,0:T(8,128)} fusion(s32[10000]{0:T(1024)} %copy-done.91, f32[10000,4]{1,0:T(8,128)} %copy.159, f32[]{:T(128)} %constant.64.clone.1), kind=kCustom, calls=%fused_computation.286 | custom fusion | flops 40000 | bytes 6288 | tf_op jit(solution)/shard_map/transpose(jvp())/scatter-add | solution.py:76
  1082.9 55.5 %scatter_custom_fusion = f32[361,4]{1,0:T(8,128)S(1)} fusion(s32[10000]{0:T(1024)} %copy-done.91, f32[10000,4]{1,0:T(8,128)} %copy.157, f32[]{:T(128)} %constant.64.clone.1), kind=kCustom, calls=%fused_computation.288 | custom fusion | flops 40000 | bytes 6288 | tf_op jit(solution)/shard_map/transpose(jvp())/scatter-add | solution.py:76
  1142.2 7.0 multiply_reduce_fusion.2
  1152.7 6.0 multiply_reduce_fusion.20
  1158.8 51.2 %all-reduce.6 = (f32[4,64]{1,0:T(4,128)}, f32[4,64]{1,0:T(4,128)}, f32[1,512]{1,0:T(1,128)S(1)}, f32[1,512]{1,0:T(1,128)S(1)}, f32[1,512]{1,0:T(1,128)S(1)}, /*i...) all-reduce(f32[4,64]{1,0:T(4,128)S(1)} %get-tuple-element.65, ...), channel_id=1, replica_groups=mesh['sp'=8,'tp'=4] {'sp'}, use_global_device_ids=true, to_apply=%region_44.45 | all-reduce | flops 11086 | bytes 88688 | tf_op jit(solution)/shard_map/psum | solution.py:323
  1210.2 11.0 all-reduce.8
  (612 shorter events, 371.9 us)
Async XLA Ops:
  7.2 33.1 %copy-start = (f32[4,64,512]{2,1,0:T(8,128)S(1)}, f32[4,64,512]{2,1,0:T(8,128)}, u32[]{:S(2)}) copy-start(f32[4,64,512]{2,1,0:T(8,128)} %param.23) | copy-start | bytes 1572868
  7.2 91.4 %all-reduce.21.cloned.1.call-start = ((), (), s32[]{:S(2)}) async-start(), calls=%async_computation | async-start | bytes 4915200 | tf_op jit(solution)/shard_map/psum | solution.py:102
  8.6 71.9 %collective-permute-start.1 = (f32[5,120]{1,0:T(8,128)S(1)}, f32[5,120]{1,0:T(8,128)S(1)}, u32[]{:S(2)}, u32[]{:S(2)}) collective-permute-start(f32[5,120]{1,0:T(8,128)S(1)} %get-tuple-element.167), channel_id=1, source_target_pairs={{4,0},{8,4},{12,8},{16,12},{20,16},{24,20},{28,24},{0,28},{5,1},{9... | collective-permute-start | bytes 7208 | tf_op jit(solution)/shard_map/ppermute | solution.py:19
  26.8 13.5 %copy-start.117 = (f32[4,64]{1,0:T(4,128)S(1)}, f32[4,64]{1,0:T(4,128)}, u32[]{:S(2)}) copy-start(f32[4,64]{1,0:T(4,128)} %param.21) | copy-start | bytes 3076
  26.8 13.5 %copy-start.173 = (f32[4,64]{1,0:T(4,128)S(1)}, f32[4,64]{1,0:T(4,128)}, u32[]{:S(2)}) copy-start(f32[4,64]{1,0:T(4,128)} %param.22) | copy-start | bytes 3076
  28.9 15.5 %copy-start.18 = (f32[1200,4,64]{0,2,1:T(8,128)}, f32[1200,4,64]{0,2,1:T(8,128)S(1)}, u32[]{:S(2)}) copy-start(f32[1200,4,64]{0,2,1:T(8,128)S(1)} %reshape.680) | copy-start | bytes 3686404
  44.4 172.0 %all-reduce.23.cloned.1.call-start = ((), (), s32[]{:S(2)}) async-start(), calls=%async_computation.1 | async-start | bytes 4915200 | tf_op jit(solution)/shard_map/psum | solution.py:102
  45.8 55.8 %copy-start.133 = (f32[1,512]{1,0:T(1,128)}, f32[1,512]{1,0:T(1,128)S(1)}, u32[]{:S(2)}) copy-start(f32[1,512]{1,0:T(1,128)S(1)} %get-tuple-element.181) | copy-start | bytes 6148
  46.4 55.2 %copy-start.177 = (f32[1,512]{1,0:T(1,128)}, f32[1,512]{1,0:T(1,128)S(1)}, u32[]{:S(2)}) copy-start(f32[1,512]{1,0:T(1,128)S(1)} %get-tuple-element.183) | copy-start | bytes 6148
  158.9 137.0 %all-reduce.25.cloned.1.call-start = ((), (), s32[]{:S(2)}) async-start(), calls=%async_computation.2 | async-start | bytes 4915200 | tf_op jit(solution)/shard_map/psum | solution.py:102
  160.0 59.2 %copy-start.145 = (f32[1,512]{1,0:T(1,128)}, f32[1,512]{1,0:T(1,128)S(1)}, u32[]{:S(2)}) copy-start(f32[1,512]{1,0:T(1,128)S(1)} %get-tuple-element.179) | copy-start | bytes 6148
  160.6 59.2 %copy-start.138 = (f32[1,512]{1,0:T(1,128)}, f32[1,512]{1,0:T(1,128)S(1)}, u32[]{:S(2)}) copy-start(f32[1,512]{1,0:T(1,128)S(1)} %get-tuple-element.173) | copy-start | bytes 6148
  161.2 58.6 %copy-start.181 = (f32[1,512]{1,0:T(1,128)}, f32[1,512]{1,0:T(1,128)S(1)}, u32[]{:S(2)}) copy-start(f32[1,512]{1,0:T(1,128)S(1)} %get-tuple-element.175) | copy-start | bytes 6148
  219.2 11.0 copy-start.94
  219.7 10.5 copy-start.107
  219.8 10.5 copy-start.121
  220.8 11.8 copy-start.44
  238.4 231.1 %all-reduce.27.cloned.1.call-start = ((), (), s32[]{:S(2)}) async-start(), calls=%async_computation.3 | async-start | bytes 4915200 | tf_op jit(solution)/shard_map/psum | solution.py:102
  239.7 58.3 %copy-start.147 = (f32[1,512]{1,0:T(1,128)}, f32[1,512]{1,0:T(1,128)S(1)}, u32[]{:S(2)}) copy-start(f32[1,512]{1,0:T(1,128)S(1)} %get-tuple-element.171) | copy-start | bytes 6148
  309.5 34.0 %collective-permute-start = (f32[5,120,384]{2,1,0:T(8,128)}, f32[5,120,384]{2,1,0:T(8,128)}, u32[]{:S(2)}, u32[]{:S(2)}) collective-permute-start(f32[5,120,384]{2,1,0:T(8,128)} %slice.241), channel_id=1, source_target_pairs={{4,0},{8,4},{12,8},{16,12},{20,16},{24,20},{28,24},{0,28},{5,1},{9... | collective-permute-start | bytes 2764808 | tf_op jit(solution)/shard_map/ppermute | solution.py:19
  394.7 17.2 %copy-start.55 = (f32[2,128,512]{2,1,0:T(8,128)S(1)}, f32[2,128,512]{2,1,0:T(8,128)}, u32[]{:S(2)}) copy-start(f32[2,128,512]{2,1,0:T(8,128)} %param.29) | copy-start | bytes 1572868
  398.7 11.4 collective-permute-start.2
  415.6 80.4 %all-gather.2.cloned.1.call-start = ((), (), s32[]{:S(2)}) async-start(), calls=%async_computation.4 | async-start | bytes 3072000 | tf_op jit(solution)/shard_map/all_gather | solution.py:302
  416.2 153.5 %all-reduce.29.cloned.1.call-start = ((), (), s32[]{:S(2)}) async-start(), calls=%async_computation.5 | async-start | bytes 4915200 | tf_op jit(solution)/shard_map/psum | solution.py:106
  496.0 10.7 copy-start.58
  512.3 227.9 %all-reduce.31.cloned.1.call-start = ((), (), s32[]{:S(2)}) async-start(), calls=%async_computation.6 | async-start | bytes 4915200 | tf_op jit(solution)/shard_map/psum | solution.py:106
  576.5 12.9 %copy-start.10 = (f32[1200,512]{1,0:T(8,128)}, f32[1200,512]{1,0:T(8,128)S(1)}, u32[]{:S(2)}) copy-start(f32[1200,512]{1,0:T(8,128)S(1)} %get-tuple-element.127) | copy-start | bytes 7372804
  578.7 10.7 collective-permute-start.3
  645.1 27.0 %copy-start.32 = (f32[10,120,384]{2,1,0:T(8,128)S(1)}, f32[10,120,384]{2,1,0:T(8,128)}, u32[]{:S(2)}) copy-start(f32[10,120,384]{2,1,0:T(8,128)} %reshape.690) | copy-start | bytes 5529604
  647.4 24.7 %collective-permute-start.4 = (f32[5,120,384]{2,1,0:T(8,128)S(1)}, f32[5,120,384]{2,1,0:T(8,128)S(1)}, u32[]{:S(2)}, u32[]{:S(2)}) collective-permute-start(f32[5,120,384]{2,1,0:T(8,128)S(1)} %fusion.135), channel_id=1, source_target_pairs={{28,0},{0,4},{4,8},{8,12},{12,16},{16,20},{20,24},{24,28},{29,1},{... | collective-permute-start | bytes 2764808 | tf_op jit(solution)/shard_map/ppermute | solution.py:19
  684.9 55.4 %copy-start.97 = (f32[1200]{0:T(1024)S(1)}, f32[1200]{0:T(1024)}, u32[]{:S(2)}) copy-start(f32[1200]{0:T(1024)} %copy-done.96) | copy-start | bytes 14404
  684.9 55.4 %copy-start.125 = (f32[1200]{0:T(1024)S(1)}, f32[1200]{0:T(1024)}, u32[]{:S(2)}) copy-start(f32[1200]{0:T(1024)} %copy-done.124) | copy-start | bytes 14404
  684.9 59.5 %copy-start.110 = (f32[1200]{0:T(1024)S(1)}, f32[1200]{0:T(1024)}, u32[]{:S(2)}) copy-start(f32[1200]{0:T(1024)} %copy-done.109) | copy-start | bytes 14404
  684.9 135.2 %all-reduce.33.cloned.1.call-start = ((), (), s32[]{:S(2)}) async-start(), calls=%async_computation.7 | async-start | bytes 4915200 | tf_op jit(solution)/shard_map/psum | solution.py:106
  747.0 8.6 copy-start.13
  762.6 231.9 %all-reduce.37.cloned.1.call-start = ((), (), s32[]{:S(2)}) async-start(), calls=%async_computation.9 | async-start | bytes 9830400 | tf_op jit(solution)/shard_map/psum | solution.py:102
  763.7 56.4 %copy-start.95 = (f32[1200]{0:T(1024)S(1)}, f32[1200]{0:T(1024)}, u32[]{:S(2)}) copy-start(f32[1200]{0:T(1024)} %copy-done.94) | copy-start | bytes 14404
  772.0 51.5 %copy-start.108 = (f32[1200]{0:T(1024)S(1)}, f32[1200]{0:T(1024)}, u32[]{:S(2)}) copy-start(f32[1200]{0:T(1024)} %copy-done.107) | copy-start | bytes 14404
  896.9 349.2 %all-reduce.35.cloned.1.call-start = ((), (), s32[]{:S(2)}) async-start(), calls=%async_computation.8 | async-start | bytes 13631488 | tf_op jit(solution)/shard_map/psum | solution.py:323
  897.5 8.4 copy-start.17
  897.5 8.4 copy-start.30
  906.0 9.8 copy-start.33
  915.9 11.9 copy-start.29
  1013.5 63.1 %copy-start.104 = (f32[6,8,100]{2,1,0:T(8,128)S(1)}, f32[6,8,100]{2,1,0:T(8,128)}, u32[]{:S(2)}) copy-start(f32[6,8,100]{2,1,0:T(8,128)} %copy-done.103) | copy-start | bytes 57604
  1079.4 62.8 %copy-start.144 = (f32[1,512]{1,0:T(1,128)S(1)}, f32[1,512]{1,0:T(1,128)}, u32[]{:S(2)}) copy-start(f32[1,512]{1,0:T(1,128)} %get-tuple-element.178) | copy-start | bytes 6148
  1079.5 62.7 %copy-start.146 = (f32[1,512]{1,0:T(1,128)S(1)}, f32[1,512]{1,0:T(1,128)}, u32[]{:S(2)}) copy-start(f32[1,512]{1,0:T(1,128)} %copy-done.145) | copy-start | bytes 6148
  1079.5 62.7 %copy-start.148 = (f32[1,512]{1,0:T(1,128)S(1)}, f32[1,512]{1,0:T(1,128)}, u32[]{:S(2)}) copy-start(f32[1,512]{1,0:T(1,128)} %copy-done.147) | copy-start | bytes 6148
  1079.5 62.7 %copy-start.164 = (f32[1,512]{1,0:T(1,128)S(1)}, f32[1,512]{1,0:T(1,128)}, u32[]{:S(2)}) copy-start(f32[1,512]{1,0:T(1,128)} %get-tuple-element.170) | copy-start | bytes 6148
  (153 other events, 597.6 us)
Sparse Core Ops, SparseCore 0:
  44.5 54.0 all-reduce.20
  159.1 57.3 all-reduce.22
  238.6 57.3 all-reduce.24
  415.7 53.8 all-reduce.26
  470.9 25.0 all-gather.1
  512.4 57.2 all-reduce.28
  685.0 55.1 all-reduce.30
  762.7 57.3 all-reduce.32
  897.0 97.4 all-reduce.36
  1005.2 240.7 all-reduce.34
where the time goes:
time: 1270 us; the launch traced here: 1260 us
  waiting for transfers between devices  451 us (36%)
  local copies, waits for them, and re-layouts  279 us (22%)
  matrix products  214 us (17%)
  other arithmetic  211 us (17%)
  blocking collectives  72.8 us (6%)
  starting transfers between devices  17.9 us (1%)
  between operations  17.3 us (1%)
    psum x5, waiting for transfers between devices, branch_total(): return lax.psum(partial_value, 'tp')  233 us
    psum x3, waiting for transfers between devices, input_total(): return lax.psum(partial_value, 'tp')  160 us
    scatter-add x2, other arithmetic, local_attention(): bias_grid = jnp.transpose(table_here[bias_index], (2, 0, 1))  112 us
    psum x1, blocking collectives, shards(): lax.psum((early_grads[0], early_grads[1], early_grads[2], early_grads[3],...  51.2 us
    unnamed x384, local copies, waits for them, and re-layouts  47.3 us
    gather x6, local copies, waits for them, and re-layouts, local_attention(): bias_grid = jnp.transpose(table_here[bias_index], (2, 0, 1))  46.7 us
    ppermute x5, waiting for transfers between devices, passed_along(): return lax.ppermute(block, axis, route)  41.2 us
    dot_general x6, matrix products, window_attention(): return jnp.einsum('whqk,wkhd->wqhd', weights, value_rows, precision=highest)  29.6 us
  transfers between devices with their start and end apart: 15, of which 13 were waited for; matrix products, arithmetic and copies ran while one was open for 26% of the time, Pallas kernels for 0%

commit v1 on v0

--- a/solution.py
+++ b/solution.py
@@ -103,7 +103,7 @@
 
 
 def input_total(partial_value):
-    return lax.psum(partial_value, "tp")
+    return jnp.sum(lax.all_gather(partial_value, "tp"), axis=0)
 
 
 def shards(

time: 1270 us -> 1360 us (1.071)
  other arithmetic: 211 us -> 257 us
  waiting for transfers between devices: 451 us -> 490 us
    all_gather x0 -> x4, waiting for transfers between devices: none -> 207 us  [input_total(): return jnp.sum(lax.all_gather(partial_value, 'tp'), axis=0)]
    psum x3 -> x0, waiting for transfers between devices: 160 us -> none  [input_total(): return lax.psum(partial_value, 'tp')]
    reduce_sum x1 -> x4, other arithmetic: 7 us -> 27 us  [input_total(): return jnp.sum(lax.all_gather(partial_value, 'tp'), axis=0)]
    reduce_sum x4 -> x8, other arithmetic: 15.6 us -> 33.8 us  [layer_norm(): return center * lax.rsqrt(spread + epsilon) * gain_row + offset]
    unnamed x384 -> x348, local copies, waits for them, and re-layouts: 47.3 us -> 47.3 us
  transfers between devices with their start and end apart: 15 -> 16, of which waited for: 13 -> 13; matrix products, arithmetic and copies ran while one was open for 26% -> 26% of each run, Pallas kernels for 0% -> 0%
where the time goes in v1:
time: 1360 us; the launch traced here: 1350 us
  waiting for transfers between devices  490 us (36%)
  local copies, waits for them, and re-layouts  278 us (20%)
  other arithmetic  257 us (19%)
  matrix products  214 us (16%)
  blocking collectives  74.2 us (5%)
  between operations  17.2 us (1%)
  starting transfers between devices  17 us (1%)
    psum x5, waiting for transfers between devices, branch_total(): return lax.psum(partial_value, 'tp')  231 us
    all_gather x4, waiting for transfers between devices, input_total(): return jnp.sum(lax.all_gather(partial_value, 'tp'), axis=0)  207 us
    scatter-add x2, other arithmetic, local_attention(): bias_grid = jnp.transpose(table_here[bias_index], (2, 0, 1))  112 us
    psum x1, blocking collectives, shards(): lax.psum((early_grads[0], early_grads[1], early_grads[2], early_grads[3],...  52.3 us
    unnamed x348, local copies, waits for them, and re-layouts  47.3 us
    gather x6, local copies, waits for them, and re-layouts, local_attention(): bias_grid = jnp.transpose(table_here[bias_index], (2, 0, 1))  46.4 us
    ppermute x5, waiting for transfers between devices, passed_along(): return lax.ppermute(block, axis, route)  41.2 us
    reduce_sum x8, other arithmetic, layer_norm(): return center * lax.rsqrt(spread + epsilon) * gain_row + offset  33.8 us
  transfers between devices with their start and end apart: 16, of which 13 were waited for; matrix products, arithmetic and copies ran while one was open for 26% of the time, Pallas kernels for 0%

profile of v1, /device:TPU:0, one launch (start us, length us, event | category | flops | bytes accessed | tf_op | source)
XLA Modules:
  0.0 1348.2 jit_solution(1650888553545840373)
XLA Ops:
  8.6 6.0 collective-permute-start.1
  16.5 6.9 fusion.220
  29.1 10.6 all-reduce.9
  45.4 7.3 gather_fusion.1
  53.6 19.5 %gather_fusion = f32[10000,4]{1,0:T(8,128)} fusion(f32[361,4]{1,0:T(8,128)S(1)} %bitcast.331, s32[10240]{0:T(1024)S(1)} %pad_clamp_fusion), kind=kCustom, calls=%fused_computation | custom fusion | bytes 360000 | tf_op jit(solution)/shard_map/gather | solution.py:76
  79.8 18.8 %all-reduce.17.cloned.1.call-done = f32[1200,512]{1,0:T(8,128)} async-done(((f32[1200,512]{1,0:T(8,128)}), f32[1200,512]{1,0:T(8,128)}) %all-reduce.17.cloned.1.call-update) | async-done | bytes 2457616 | tf_op jit(solution)/shard_map/psum | solution.py:102
  117.2 7.2 reshape_reshape.21
  124.4 7.1 fusion.234
  161.6 54.9 %all-reduce.19.cloned.1.call-done = f32[1200,512]{1,0:T(8,128)} async-done(((f32[1200,512]{1,0:T(8,128)}), f32[1200,512]{1,0:T(8,128)}) %all-reduce.19.cloned.1.call-update) | async-done | bytes 2457616 | tf_op jit(solution)/shard_map/psum | solution.py:102
  220.9 9.4 fusion
  232.5 6.0 fusion.120
  239.8 56.2 %all-reduce.21.cloned.1.call-done = f32[1200,512]{1,0:T(8,128)} async-done(((f32[1200,512]{1,0:T(8,128)}), f32[1200,512]{1,0:T(8,128)}) %all-reduce.21.cloned.1.call-update) | async-done | bytes 2457616 | tf_op jit(solution)/shard_map/psum | solution.py:102
  314.0 19.5 %gather_fusion.2 = f32[10000,4]{1,0:T(8,128)} fusion(f32[361,4]{1,0:T(8,128)S(1)} %bitcast.330, s32[10240]{0:T(1024)S(1)} %pad_clamp_fusion), kind=kCustom, calls=%fused_computation.2 | custom fusion | bytes 360000 | tf_op jit(solution)/shard_map/gather | solution.py:76
  353.3 6.8 reshape_reshape.24
  360.1 6.4 fusion.233
  398.6 11.3 collective-permute-done.2
  416.4 52.9 %all-reduce.23.cloned.1.call-done = f32[1200,512]{1,0:T(8,128)} async-done(((f32[1200,512]{1,0:T(8,128)}), f32[1200,512]{1,0:T(8,128)}) %all-reduce.23.cloned.1.call-update) | async-done | bytes 2457616 | tf_op jit(solution)/shard_map/psum | solution.py:102
  474.6 11.1 fusion.1
  485.7 10.1 all-gather.10.cloned.1.call-done
  495.8 9.2 fusion.248
  512.2 8.2 fusion.111
  521.9 56.7 %all-gather.12.cloned.1.call-done = f32[4800,512]{1,0:T(8,128)} async-done(((f32[1200,512]{1,0:T(8,128)}), f32[4800,512]{1,0:T(8,128)}) %all-gather.12.cloned.1.call-update) | async-done | bytes 9830416 | tf_op jit(solution)/shard_map/all_gather | solution.py:106
  578.6 6.7 reduce_sum.555
  590.2 48.0 %all-reduce.25.cloned.1.call-done = f32[1200,512]{1,0:T(8,128)} async-done(((f32[1200,512]{1,0:T(8,128)}), f32[1200,512]{1,0:T(8,128)}) %all-reduce.25.cloned.1.call-update) | async-done | bytes 2457616 | tf_op jit(solution)/shard_map/psum | solution.py:102
  638.3 8.8 fusion.229
  672.5 6.2 convolution_bitcast_fusion.7
  695.1 7.0 copy.141
  702.1 7.2 reshape.689
  719.6 24.0 %collective-permute-done.4 = f32[5,120,384]{2,1,0:T(8,128)S(1)} collective-permute-done((f32[5,120,384]{2,1,0:T(8,128)S(1)}, f32[5,120,384]{2,1,0:T(8,128)S(1)}, u32[]{:S(2)}, u32[]{:S(2)}) %collective-permute-start.4) | collective-permute-done | bytes 921632 | tf_op jit(solution)/shard_map/ppermute | solution.py:19
  749.0 7.4 convolution_bitcast_fusion.2
  756.6 64.3 %all-gather.14.cloned.1.call-done = f32[4800,512]{1,0:T(8,128)} async-done(((f32[1200,512]{1,0:T(8,128)}), f32[4800,512]{1,0:T(8,128)}) %all-gather.14.cloned.1.call-update) | async-done | bytes 9830416 | tf_op jit(solution)/shard_map/all_gather | solution.py:106
  820.9 6.7 reduce_sum.567
  851.5 65.3 %all-gather.16.cloned.1.call-done = f32[4800,512]{1,0:T(8,128)} async-done(((f32[1200,512]{1,0:T(8,128)}), f32[4800,512]{1,0:T(8,128)}) %all-gather.16.cloned.1.call-update) | async-done | bytes 9830416 | tf_op jit(solution)/shard_map/all_gather | solution.py:106
  916.8 6.7 reduce_sum.573
  948.3 6.2 convolution_bitcast_fusion.6
  970.5 7.1 copy.150
  977.6 7.2 reshape.694
  993.0 7.3 convolution_bitcast_fusion.1
  1001.1 8.4 fusion.49
  1009.6 7.7 convolution_bitcast_fusion.3
  1019.8 6.2 fusion.56
  1046.1 20.9 %all-gather.18.cloned.1.call-done = f32[4800,512]{1,0:T(8,128)} async-done(((f32[1200,512]{1,0:T(8,128)}), f32[4800,512]{1,0:T(8,128)}) %all-gather.18.cloned.1.call-update) | async-done | bytes 9830416 | tf_op jit(solution)/shard_map/all_gather | solution.py:106
  1067.1 6.7 reduce_sum.582
  1105.7 56.2 %scatter_custom_fusion.1 = f32[361,4]{1,0:T(8,128)} fusion(s32[10000]{0:T(1024)} %copy-done.88, f32[10000,4]{1,0:T(8,128)} %copy.159, f32[]{:T(128)} %constant.64.clone.1), kind=kCustom, calls=%fused_computation.286 | custom fusion | flops 40000 | bytes 6288 | tf_op jit(solution)/shard_map/transpose(jvp())/scatter-add | solution.py:76
  1176.3 55.4 %scatter_custom_fusion = f32[361,4]{1,0:T(8,128)S(1)} fusion(s32[10000]{0:T(1024)} %copy-done.88, f32[10000,4]{1,0:T(8,128)} %copy.157, f32[]{:T(128)} %constant.64.clone.1), kind=kCustom, calls=%fused_computation.288 | custom fusion | flops 40000 | bytes 6288 | tf_op jit(solution)/shard_map/transpose(jvp())/scatter-add | solution.py:76
  1244.8 6.1 multiply_reduce_fusion.20
  1251.0 52.3 %all-reduce.6 = (f32[4,64]{1,0:T(4,128)}, f32[4,64]{1,0:T(4,128)}, f32[1,512]{1,0:T(1,128)S(1)}, f32[1,512]{1,0:T(1,128)S(1)}, f32[1,512]{1,0:T(1,128)S(1)}, /*i...) all-reduce(f32[4,64]{1,0:T(4,128)S(1)} %get-tuple-element.65, ...), channel_id=1, replica_groups=mesh['sp'=8,'tp'=4] {'sp'}, use_global_device_ids=true, to_apply=%region_44.45 | all-reduce | flops 11086 | bytes 88688 | tf_op jit(solution)/shard_map/psum | solution.py:323
  1303.5 11.3 all-reduce.8
  (586 shorter events, 410.9 us)
Async XLA Ops:
  7.2 33.1 %copy-start = (f32[4,64,512]{2,1,0:T(8,128)S(1)}, f32[4,64,512]{2,1,0:T(8,128)}, u32[]{:S(2)}) copy-start(f32[4,64,512]{2,1,0:T(8,128)} %param.23) | copy-start | bytes 1572868
  7.2 91.4 %all-reduce.17.cloned.1.call-start = ((), (), s32[]{:S(2)}) async-start(), calls=%async_computation | async-start | bytes 4915200 | tf_op jit(solution)/shard_map/psum | solution.py:102
  8.6 69.1 %collective-permute-start.1 = (f32[5,120]{1,0:T(8,128)S(1)}, f32[5,120]{1,0:T(8,128)S(1)}, u32[]{:S(2)}, u32[]{:S(2)}) collective-permute-start(f32[5,120]{1,0:T(8,128)S(1)} %get-tuple-element.167), channel_id=1, source_target_pairs={{4,0},{8,4},{12,8},{16,12},{20,16},{24,20},{28,24},{0,28},{5,1},{9... | collective-permute-start | bytes 7208 | tf_op jit(solution)/shard_map/ppermute | solution.py:19
  26.8 13.5 %copy-start.114 = (f32[4,64]{1,0:T(4,128)S(1)}, f32[4,64]{1,0:T(4,128)}, u32[]{:S(2)}) copy-start(f32[4,64]{1,0:T(4,128)} %param.21) | copy-start | bytes 3076
  26.8 13.5 %copy-start.155 = (f32[4,64]{1,0:T(4,128)S(1)}, f32[4,64]{1,0:T(4,128)}, u32[]{:S(2)}) copy-start(f32[4,64]{1,0:T(4,128)} %param.22) | copy-start | bytes 3076
  28.9 15.5 %copy-start.17 = (f32[1200,4,64]{0,2,1:T(8,128)}, f32[1200,4,64]{0,2,1:T(8,128)S(1)}, u32[]{:S(2)}) copy-start(f32[1200,4,64]{0,2,1:T(8,128)S(1)} %reshape.680) | copy-start | bytes 3686404
  44.4 172.1 %all-reduce.19.cloned.1.call-start = ((), (), s32[]{:S(2)}) async-start(), calls=%async_computation.1 | async-start | bytes 4915200 | tf_op jit(solution)/shard_map/psum | solution.py:102
  44.9 56.7 %copy-start.125 = (f32[1,512]{1,0:T(1,128)}, f32[1,512]{1,0:T(1,128)S(1)}, u32[]{:S(2)}) copy-start(f32[1,512]{1,0:T(1,128)S(1)} %get-tuple-element.181) | copy-start | bytes 6148
  44.9 253.7 %copy-start.127 = (f32[1,512]{1,0:T(1,128)}, f32[1,512]{1,0:T(1,128)S(1)}, u32[]{:S(2)}) copy-start(f32[1,512]{1,0:T(1,128)S(1)} %get-tuple-element.180) | copy-start | bytes 6148
  44.9 56.6 %copy-start.159 = (f32[1,512]{1,0:T(1,128)}, f32[1,512]{1,0:T(1,128)S(1)}, u32[]{:S(2)}) copy-start(f32[1,512]{1,0:T(1,128)S(1)} %get-tuple-element.183) | copy-start | bytes 6148
  45.0 253.7 %copy-start.161 = (f32[1,512]{1,0:T(1,128)}, f32[1,512]{1,0:T(1,128)S(1)}, u32[]{:S(2)}) copy-start(f32[1,512]{1,0:T(1,128)S(1)} %get-tuple-element.182) | copy-start | bytes 6148
  45.4 7.6 copy-start.88
  138.9 7.4 copy-start.70
  159.0 137.0 %all-reduce.21.cloned.1.call-start = ((), (), s32[]{:S(2)}) async-start(), calls=%async_computation.2 | async-start | bytes 4915200 | tf_op jit(solution)/shard_map/psum | solution.py:102
  159.8 59.4 %copy-start.135 = (f32[1,512]{1,0:T(1,128)}, f32[1,512]{1,0:T(1,128)S(1)}, u32[]{:S(2)}) copy-start(f32[1,512]{1,0:T(1,128)S(1)} %get-tuple-element.179) | copy-start | bytes 6148
  160.4 59.4 %copy-start.130 = (f32[1,512]{1,0:T(1,128)}, f32[1,512]{1,0:T(1,128)S(1)}, u32[]{:S(2)}) copy-start(f32[1,512]{1,0:T(1,128)S(1)} %get-tuple-element.173) | copy-start | bytes 6148
  161.0 58.8 %copy-start.163 = (f32[1,512]{1,0:T(1,128)}, f32[1,512]{1,0:T(1,128)S(1)}, u32[]{:S(2)}) copy-start(f32[1,512]{1,0:T(1,128)S(1)} %get-tuple-element.175) | copy-start | bytes 6148
  219.3 11.0 copy-start.93
  219.8 10.5 copy-start.105
  219.8 10.5 copy-start.118
  220.9 11.6 copy-start.42
  238.5 230.8 %all-reduce.23.cloned.1.call-start = ((), (), s32[]{:S(2)}) async-start(), calls=%async_computation.3 | async-start | bytes 4915200 | tf_op jit(solution)/shard_map/psum | solution.py:102
  239.8 58.3 %copy-start.136 = (f32[1,512]{1,0:T(1,128)}, f32[1,512]{1,0:T(1,128)S(1)}, u32[]{:S(2)}) copy-start(f32[1,512]{1,0:T(1,128)S(1)} %get-tuple-element.171) | copy-start | bytes 6148
  309.6 33.9 %collective-permute-start = (f32[5,120,384]{2,1,0:T(8,128)}, f32[5,120,384]{2,1,0:T(8,128)}, u32[]{:S(2)}, u32[]{:S(2)}) collective-permute-start(f32[5,120,384]{2,1,0:T(8,128)} %slice.241), channel_id=1, source_target_pairs={{4,0},{8,4},{12,8},{16,12},{20,16},{24,20},{28,24},{0,28},{5,1},{9... | collective-permute-start | bytes 2764808 | tf_op jit(solution)/shard_map/ppermute | solution.py:19
  375.2 7.4 copy-start.72
  394.6 17.2 %copy-start.53 = (f32[2,128,512]{2,1,0:T(8,128)S(1)}, f32[2,128,512]{2,1,0:T(8,128)}, u32[]{:S(2)}) copy-start(f32[2,128,512]{2,1,0:T(8,128)} %param.29) | copy-start | bytes 1572868
  398.5 11.4 collective-permute-start.2
  415.3 80.4 %all-gather.10.cloned.1.call-start = ((), (), s32[]{:S(2)}) async-start(), calls=%async_computation.5 | async-start | bytes 3072000 | tf_op jit(solution)/shard_map/all_gather | solution.py:302
  415.9 162.7 %all-gather.12.cloned.1.call-start = ((), (), s32[]{:S(2)}) async-start(), calls=%async_computation.6 | async-start | bytes 12288000 | tf_op jit(solution)/shard_map/all_gather | solution.py:106
  495.8 10.7 copy-start.56
  512.0 126.3 %all-reduce.25.cloned.1.call-start = ((), (), s32[]{:S(2)}) async-start(), calls=%async_computation.4 | async-start | bytes 4915200 | tf_op jit(solution)/shard_map/psum | solution.py:102
  520.4 300.5 %all-gather.14.cloned.1.call-start = ((), (), s32[]{:S(2)}) async-start(), calls=%async_computation.7 | async-start | bytes 12288000 | tf_op jit(solution)/shard_map/all_gather | solution.py:106
  638.3 8.8 copy-start.14
  648.0 12.9 copy-start.8
  650.2 10.7 collective-permute-start.3
  716.6 27.0 %copy-start.34 = (f32[10,120,384]{2,1,0:T(8,128)S(1)}, f32[10,120,384]{2,1,0:T(8,128)}, u32[]{:S(2)}) copy-start(f32[10,120,384]{2,1,0:T(8,128)} %reshape.690) | copy-start | bytes 5529604
  719.0 24.7 %collective-permute-start.4 = (f32[5,120,384]{2,1,0:T(8,128)S(1)}, f32[5,120,384]{2,1,0:T(8,128)S(1)}, u32[]{:S(2)}, u32[]{:S(2)}) collective-permute-start(f32[5,120,384]{2,1,0:T(8,128)S(1)} %fusion.135), channel_id=1, source_target_pairs={{28,0},{0,4},{4,8},{8,12},{12,16},{16,20},{20,24},{24,28},{29,1},{... | collective-permute-start | bytes 2764808 | tf_op jit(solution)/shard_map/ppermute | solution.py:19
  756.3 160.5 %all-gather.16.cloned.1.call-start = ((), (), s32[]{:S(2)}) async-start(), calls=%async_computation.8 | async-start | bytes 12288000 | tf_op jit(solution)/shard_map/all_gather | solution.py:106
  834.3 8.6 copy-start.11
  850.2 216.9 %all-gather.18.cloned.1.call-start = ((), (), s32[]{:S(2)}) async-start(), calls=%async_computation.9 | async-start | bytes 12288000 | tf_op jit(solution)/shard_map/all_gather | solution.py:106
  1000.4 331.5 %all-reduce.27.cloned.1.call-start = ((), (), s32[]{:S(2)}) async-start(), calls=%async_computation.10 | async-start | bytes 13631488 | tf_op jit(solution)/shard_map/psum | solution.py:323
  1001.1 8.4 copy-start.15
  1001.1 8.4 copy-start.29
  1009.5 7.8 copy-start.10
  1009.6 7.8 copy-start.47
  1009.6 10.2 copy-start.35
  1019.8 12.2 copy-start.28
  1032.0 8.2 copy-start.36
  (136 other events, 512.0 us)
Sparse Core Ops, SparseCore 0:
  44.5 54.0 all-reduce.16
  159.1 57.3 all-reduce.18
  238.6 57.3 all-reduce.20
  415.5 53.8 all-reduce.22
  470.7 25.0 all-gather.9
  512.1 66.4 all-gather.11
  581.0 57.2 all-reduce.24
  756.5 64.3 all-gather.13
  850.3 66.4 all-gather.15
  1000.5 66.4 all-gather.17
  1084.1 240.5 all-reduce.26
